TPU v7x, 512 devices: a whole 4x8x8 slice. The times are simulated.
512 devices in a mesh: section: 4 (over x), dom: 128 (over z, y, core).
Axes of the slice: x: 4, y: 8, z: 8, core: 2. Of those that a mesh axis runs over, the one named last changes fastest.
Arguments:
- features: bfloat16 [2, 32768, 128], P(None, 'dom'), may hold values from -6 to 6
- input_weight: bfloat16 [128, 512], replicated, may hold values from -0.5 to 0.5
- layer_weights: bfloat16 [8, 512, 512], P('section'), may hold values from -0.25 to 0.25
- tiles: bfloat16 [2, 256, 4, 128, 128], P(None, 'dom'), may hold values from -0.4375 to 0.4375
- pub_ids: int32 [2, 256], P(None, 'dom'), may hold values from -1 to 1, as said below
- tile_src: int32 [2, 256, 4], P(None, 'dom'), may hold values from 0 to 5, as said below
Outputs:
- section_outputs: bfloat16 [4, 2, 32768, 512], P('section', None, 'dom')
Inputs may be any that keep to these rules, and one draw needn't show every extreme that they name: `pub_ids`: for each node group and partition, its 2 slots hold distinct local block numbers below 2 first and -1 in the unused slots after them; every partition lists at least one block, and in every node group some partition fills all 2 slots. `tile_src`: each entry names a slot of the destination block's partition: a local block below 2, or a listed (not -1) slot of the previous or the next partition; the first partition reads no previous one and the last no next one. In every node group some tile reads the last slot of a next partition.
All inputs are finite; a program needn't handle non-finite values.
Results may differ from a plain program's by a relative error of at most 0.019.
Values may be sent and summed in bfloat16 or wider, within the bound.
A program may use at most 64 MiB of HBM per device.

v0:
```python
import jax
import jax.numpy as jnp
from jax import lax
from jax.sharding import PartitionSpec as P

residual_share = 0.1
decay_theta = 0.5


def passed_along(block, axis, distance):
    devices = range(lax.axis_size(axis))
    route = [(i - distance, i) for i in devices if i - distance in devices]
    return lax.ppermute(block, axis, route)


def shards(features, input_weight, layer_weights, tiles, pub_ids, tile_src):
    groups = features.shape[0]
    node_rows = features.shape[1]
    block_count = tiles.shape[1]
    tile_count = tiles.shape[2]
    block_rows = tiles.shape[3]
    feature_width = input_weight.shape[1]
    slot_count = pub_ids.shape[1]
    layers_here = layer_weights.shape[0]
    section_index = lax.axis_index("section")
    section_total = lax.axis_size("section")
    total_steps = groups + section_total - 1
    empty_rows = jnp.zeros((node_rows, feature_width), jnp.bfloat16)
    carried_hidden = empty_rows
    carried_initial = empty_rows
    collected = jnp.zeros((groups, node_rows, feature_width), jnp.bfloat16)
    for tick in range(total_steps):
        group_index = tick - section_index
        active = (group_index >= 0) & (group_index < groups)
        clamped = jnp.clip(group_index, 0, groups - 1)
        fresh = jax.nn.relu(
            jnp.dot(
                features[min(tick, groups - 1)], input_weight, preferred_element_type=jnp.float32
            )
        ).astype(jnp.bfloat16)
        initial = jnp.where(section_index == 0, fresh, carried_initial)
        current = jnp.where(section_index == 0, fresh, carried_hidden)
        tile_block = lax.dynamic_index_in_dim(tiles, clamped, 0, keepdims=False)
        sources = lax.dynamic_index_in_dim(tile_src, clamped, 0, keepdims=False)
        listed = lax.dynamic_index_in_dim(pub_ids, clamped, 0, keepdims=False)
        for layer in range(layers_here):
            number = (section_index * layers_here + layer + 1).astype(jnp.float32)
            beta = jnp.log(decay_theta / number + 1.0)
            blocks = current.reshape(block_count, block_rows, feature_width)
            select = (listed[:, None] == jnp.arange(block_count)[None, :]).astype(jnp.bfloat16)
            packed = jnp.einsum("mn,nrd->mrd", select, blocks, preferred_element_type=jnp.float32)
            packed = packed.astype(jnp.bfloat16).reshape(slot_count * block_rows, feature_width)
            received = [passed_along(packed, "dom", offset) for offset in (1, -1)]
            table = jnp.concatenate(
                [blocks] + [piece.reshape(-1, block_rows, feature_width) for piece in received], 0
            )
            gathered = jnp.take(table, sources.reshape(-1), axis=0).reshape(
                block_count, tile_count, block_rows, feature_width
            )
            aggregate = jnp.einsum(
                "bkij,bkjd->bid", tile_block, gathered, preferred_element_type=jnp.float32
            )
            aggregate = aggregate.reshape(node_rows, feature_width)
            support = (
                (1.0 - residual_share) * aggregate + residual_share * initial.astype(jnp.float32)
            ).astype(jnp.bfloat16)
            product = jnp.dot(support, layer_weights[layer], preferred_element_type=jnp.float32)
            mixed = (1.0 - beta) * support.astype(jnp.float32) + beta * product
            current = jax.nn.relu(mixed).astype(jnp.bfloat16)
        previous = lax.dynamic_index_in_dim(collected, clamped, 0, keepdims=False)
        collected = lax.dynamic_update_index_in_dim(
            collected, jnp.where(active, current, previous), clamped, 0
        )
        if tick + 1 < total_steps:
            carried_hidden, carried_initial = passed_along((current, initial), "section", 1)
    return collected[None]


def solution(mesh):
    in_specs = (
        P(None, "dom", None),
        P(),
        P("section", None, None),
        P(None, "dom", None, None, None),
        P(None, "dom"),
        P(None, "dom", None),
    )
    out_specs = P("section", None, "dom", None)
    return jax.shard_map(shards, mesh=mesh, in_specs=in_specs, out_specs=out_specs, check_vma=False)
```

profile of v0, /device:TPU:251, one launch (start us, length us, event | category | flops | bytes accessed | tf_op | source)
XLA Modules:
  0.0 209.2 jit_solution(9078676248864521996)
XLA Ops:
  0.0 1.2 fusion.42
  1.8 5.0 %collective-permute-start = (bf16[256,512]{1,0:T(8,128)(2,1)S(1)}, bf16[256,512]{1,0:T(8,128)(2,1)S(1)}, u32[]{:S(2)}, u32[]{:S(2)}) collective-permute-start(bf16[256,512]{1,0:T(8,128)(2,1)S(1)} %bitcast.303), channel_id=1, source_target_pairs={{0,1},{1,2},{2,3},{3,4},{4,5},{5,6},{6,7},{7,8},{8,9},{9,10},{10,1... | collective-permute-start | bytes 786440 | tf_op jit(solution)/shard_map/ppermute | solution.py:13
  6.8 1.9 collective-permute-start.1
  9.0 1.1 collective-permute-done
  10.1 7.7 %collective-permute-done.1 = bf16[256,512]{1,0:T(8,128)(2,1)S(1)} collective-permute-done((bf16[256,512]{1,0:T(8,128)(2,1)S(1)}, bf16[256,512]{1,0:T(8,128)(2,1)S(1)}, u32[]{:S(2)}, u32[]{:S(2)}) %collective-permute-start.1) | collective-permute-done | bytes 262176 | tf_op jit(solution)/shard_map/ppermute | solution.py:13
  20.8 1.9 collective-permute-start.2
  22.7 2.4 %collective-permute-start.3 = (bf16[256,512]{1,0:T(8,128)(2,1)S(1)}, bf16[256,512]{1,0:T(8,128)(2,1)S(1)}, u32[]{:S(2)}, u32[]{:S(2)}) collective-permute-start(bf16[256,512]{1,0:T(8,128)(2,1)S(1)} %bitcast.306), channel_id=1, source_target_pairs={{1,0},{2,1},{3,2},{4,3},{5,4},{6,5},{7,6},{8,7},{9,8},{10,9},{11,1... | collective-permute-start | bytes 786440 | tf_op jit(solution)/shard_map/ppermute | solution.py:13
  26.0 7.7 %collective-permute-done.3 = bf16[256,512]{1,0:T(8,128)(2,1)S(1)} collective-permute-done((bf16[256,512]{1,0:T(8,128)(2,1)S(1)}, bf16[256,512]{1,0:T(8,128)(2,1)S(1)}, u32[]{:S(2)}, u32[]{:S(2)}) %collective-permute-start.3) | collective-permute-done | bytes 262176 | tf_op jit(solution)/shard_map/ppermute | solution.py:13
  36.5 3.1 %collective-permute-start.4 = (bf16[256,512]{1,0:T(8,128)(2,1)S(1)}, bf16[256,512]{1,0:T(8,128)(2,1)S(1)}, u32[]{:S(2)}, u32[]{:S(2)}) collective-permute-start(bf16[256,512]{1,0:T(8,128)(2,1)S(1)} %get-tuple-element.23), channel_id=1, source_target_pairs={{0,128},{128,256},{256,384},{1,129},{129,257},{257,385},{2,130},{1... | collective-permute-start | bytes 786440 | tf_op jit(solution)/shard_map/ppermute | solution.py:13
  39.6 2.8 %collective-permute-start.7 = (bf16[256,512]{1,0:T(8,128)(2,1)S(1)}, bf16[256,512]{1,0:T(8,128)(2,1)}, u32[]{:S(2)}, u32[]{:S(2)}) collective-permute-start(bf16[256,512]{1,0:T(8,128)(2,1)S(1)} %fusion.42), channel_id=1, source_target_pairs={{0,128},{128,256},{256,384},{1,129},{129,257},{257,385},{2,130},{1... | collective-permute-start | bytes 786440 | tf_op jit(solution)/shard_map/ppermute | solution.py:13
  42.5 3.0 %collective-permute-done.4 = bf16[256,512]{1,0:T(8,128)(2,1)S(1)} collective-permute-done((bf16[256,512]{1,0:T(8,128)(2,1)S(1)}, bf16[256,512]{1,0:T(8,128)(2,1)S(1)}, u32[]{:S(2)}, u32[]{:S(2)}) %collective-permute-start.4) | collective-permute-done | bytes 262176 | tf_op jit(solution)/shard_map/ppermute | solution.py:13
  46.3 1.9 collective-permute-start.5
  48.2 2.4 %collective-permute-start.6 = (bf16[256,512]{1,0:T(8,128)(2,1)S(1)}, bf16[256,512]{1,0:T(8,128)(2,1)S(1)}, u32[]{:S(2)}, u32[]{:S(2)}) collective-permute-start(bf16[256,512]{1,0:T(8,128)(2,1)S(1)} %bitcast.312), channel_id=1, source_target_pairs={{1,0},{2,1},{3,2},{4,3},{5,4},{6,5},{7,6},{8,7},{9,8},{10,9},{11,1... | collective-permute-start | bytes 786440 | tf_op jit(solution)/shard_map/ppermute | solution.py:13
  51.5 7.7 %collective-permute-done.6 = bf16[256,512]{1,0:T(8,128)(2,1)S(1)} collective-permute-done((bf16[256,512]{1,0:T(8,128)(2,1)S(1)}, bf16[256,512]{1,0:T(8,128)(2,1)S(1)}, u32[]{:S(2)}, u32[]{:S(2)}) %collective-permute-start.6) | collective-permute-done | bytes 262176 | tf_op jit(solution)/shard_map/ppermute | solution.py:13
  60.5 1.2 fusion.53
  62.6 1.9 collective-permute-start.8
  64.5 2.4 %collective-permute-start.9 = (bf16[256,512]{1,0:T(8,128)(2,1)S(1)}, bf16[256,512]{1,0:T(8,128)(2,1)S(1)}, u32[]{:S(2)}, u32[]{:S(2)}) collective-permute-start(bf16[256,512]{1,0:T(8,128)(2,1)S(1)} %bitcast.314), channel_id=1, source_target_pairs={{1,0},{2,1},{3,2},{4,3},{5,4},{6,5},{7,6},{8,7},{9,8},{10,9},{11,1... | collective-permute-start | bytes 786440 | tf_op jit(solution)/shard_map/ppermute | solution.py:13
  67.8 7.7 %collective-permute-done.9 = bf16[256,512]{1,0:T(8,128)(2,1)S(1)} collective-permute-done((bf16[256,512]{1,0:T(8,128)(2,1)S(1)}, bf16[256,512]{1,0:T(8,128)(2,1)S(1)}, u32[]{:S(2)}, u32[]{:S(2)}) %collective-permute-start.9) | collective-permute-done | bytes 262176 | tf_op jit(solution)/shard_map/ppermute | solution.py:13
  78.1 2.8 %collective-permute-start.10 = (bf16[256,512]{1,0:T(8,128)(2,1)S(1)}, bf16[256,512]{1,0:T(8,128)(2,1)S(1)}, u32[]{:S(2)}, u32[]{:S(2)}) collective-permute-start(bf16[256,512]{1,0:T(8,128)(2,1)S(1)} %get-tuple-element.27), channel_id=1, source_target_pairs={{0,128},{128,256},{256,384},{1,129},{129,257},{257,385},{2,130},{1... | collective-permute-start | bytes 786440 | tf_op jit(solution)/shard_map/ppermute | solution.py:13
  81.0 4.3 %collective-permute-done.10 = bf16[256,512]{1,0:T(8,128)(2,1)S(1)} collective-permute-done((bf16[256,512]{1,0:T(8,128)(2,1)S(1)}, bf16[256,512]{1,0:T(8,128)(2,1)S(1)}, u32[]{:S(2)}, u32[]{:S(2)}) %collective-permute-start.10) | collective-permute-done | bytes 262176 | tf_op jit(solution)/shard_map/ppermute | solution.py:13
  85.8 2.9 %collective-permute-start.11 = (bf16[256,512]{1,0:T(8,128)(2,1)S(1)}, bf16[256,512]{1,0:T(8,128)(2,1)S(1)}, u32[]{:S(2)}, u32[]{:S(2)}) collective-permute-start(bf16[256,512]{1,0:T(8,128)(2,1)S(1)} %bitcast.315), channel_id=1, source_target_pairs={{0,1},{1,2},{2,3},{3,4},{4,5},{5,6},{6,7},{7,8},{8,9},{9,10},{10,1... | collective-permute-start | bytes 786440 | tf_op jit(solution)/shard_map/ppermute | solution.py:13
  88.7 1.9 collective-permute-start.12
  90.7 2.8 %collective-permute-start.13 = (bf16[256,512]{1,0:T(8,128)(2,1)S(1)}, bf16[256,512]{1,0:T(8,128)(2,1)}, u32[]{:S(2)}, u32[]{:S(2)}) collective-permute-start(bf16[256,512]{1,0:T(8,128)(2,1)S(1)} %get-tuple-element.11), channel_id=1, source_target_pairs={{0,128},{128,256},{256,384},{1,129},{129,257},{257,385},{2,130},{1... | collective-permute-start | bytes 786440 | tf_op jit(solution)/shard_map/ppermute | solution.py:13
  93.5 6.2 %collective-permute-done.12 = bf16[256,512]{1,0:T(8,128)(2,1)S(1)} collective-permute-done((bf16[256,512]{1,0:T(8,128)(2,1)S(1)}, bf16[256,512]{1,0:T(8,128)(2,1)S(1)}, u32[]{:S(2)}, u32[]{:S(2)}) %collective-permute-start.12) | collective-permute-done | bytes 262176 | tf_op jit(solution)/shard_map/ppermute | solution.py:13
  101.0 1.2 fusion.51
  103.1 4.9 %collective-permute-start.14 = (bf16[256,512]{1,0:T(8,128)(2,1)S(1)}, bf16[256,512]{1,0:T(8,128)(2,1)S(1)}, u32[]{:S(2)}, u32[]{:S(2)}) collective-permute-start(bf16[256,512]{1,0:T(8,128)(2,1)S(1)} %bitcast.317), channel_id=1, source_target_pairs={{0,1},{1,2},{2,3},{3,4},{4,5},{5,6},{6,7},{7,8},{8,9},{9,10},{10,1... | collective-permute-start | bytes 786440 | tf_op jit(solution)/shard_map/ppermute | solution.py:13
  108.0 1.9 collective-permute-start.15
  111.3 7.7 %collective-permute-done.15 = bf16[256,512]{1,0:T(8,128)(2,1)S(1)} collective-permute-done((bf16[256,512]{1,0:T(8,128)(2,1)S(1)}, bf16[256,512]{1,0:T(8,128)(2,1)S(1)}, u32[]{:S(2)}, u32[]{:S(2)}) %collective-permute-start.15) | collective-permute-done | bytes 262176 | tf_op jit(solution)/shard_map/ppermute | solution.py:13
  121.6 2.8 %collective-permute-start.16 = (bf16[256,512]{1,0:T(8,128)(2,1)S(1)}, bf16[256,512]{1,0:T(8,128)(2,1)S(1)}, u32[]{:S(2)}, u32[]{:S(2)}) collective-permute-start(bf16[256,512]{1,0:T(8,128)(2,1)S(1)} %get-tuple-element.29), channel_id=1, source_target_pairs={{0,128},{128,256},{256,384},{1,129},{129,257},{257,385},{2,130},{1... | collective-permute-start | bytes 786440 | tf_op jit(solution)/shard_map/ppermute | solution.py:13
  124.5 4.5 %collective-permute-done.16 = bf16[256,512]{1,0:T(8,128)(2,1)S(1)} collective-permute-done((bf16[256,512]{1,0:T(8,128)(2,1)S(1)}, bf16[256,512]{1,0:T(8,128)(2,1)S(1)}, u32[]{:S(2)}, u32[]{:S(2)}) %collective-permute-start.16) | collective-permute-done | bytes 262176 | tf_op jit(solution)/shard_map/ppermute | solution.py:13
  129.5 2.6 %collective-permute-start.17 = (bf16[256,512]{1,0:T(8,128)(2,1)S(1)}, bf16[256,512]{1,0:T(8,128)(2,1)S(1)}, u32[]{:S(2)}, u32[]{:S(2)}) collective-permute-start(bf16[256,512]{1,0:T(8,128)(2,1)S(1)} %bitcast.307), channel_id=1, source_target_pairs={{0,1},{1,2},{2,3},{3,4},{4,5},{5,6},{6,7},{7,8},{8,9},{9,10},{10,1... | collective-permute-start | bytes 786440 | tf_op jit(solution)/shard_map/ppermute | solution.py:13
  132.1 1.9 collective-permute-start.18
  134.2 3.0 %collective-permute-start.19 = (bf16[256,512]{1,0:T(8,128)(2,1)S(1)}, bf16[256,512]{1,0:T(8,128)(2,1)}, u32[]{:S(2)}, u32[]{:S(2)}) collective-permute-start(bf16[256,512]{1,0:T(8,128)(2,1)S(1)} %get-tuple-element.9), channel_id=1, source_target_pairs={{0,128},{128,256},{256,384},{1,129},{129,257},{257,385},{2,130},{1... | collective-permute-start | bytes 786440 | tf_op jit(solution)/shard_map/ppermute | solution.py:13
  137.2 6.0 %collective-permute-done.18 = bf16[256,512]{1,0:T(8,128)(2,1)S(1)} collective-permute-done((bf16[256,512]{1,0:T(8,128)(2,1)S(1)}, bf16[256,512]{1,0:T(8,128)(2,1)S(1)}, u32[]{:S(2)}, u32[]{:S(2)}) %collective-permute-start.18) | collective-permute-done | bytes 262176 | tf_op jit(solution)/shard_map/ppermute | solution.py:13
  144.4 1.9 fusion.49
  147.1 5.0 %collective-permute-start.20 = (bf16[256,512]{1,0:T(8,128)(2,1)S(1)}, bf16[256,512]{1,0:T(8,128)(2,1)S(1)}, u32[]{:S(2)}, u32[]{:S(2)}) collective-permute-start(bf16[256,512]{1,0:T(8,128)(2,1)S(1)} %bitcast.319), channel_id=1, source_target_pairs={{0,1},{1,2},{2,3},{3,4},{4,5},{5,6},{6,7},{7,8},{8,9},{9,10},{10,1... | collective-permute-start | bytes 786440 | tf_op jit(solution)/shard_map/ppermute | solution.py:13
  152.1 1.9 collective-permute-start.21
  154.1 1.3 collective-permute-done.20
  155.4 7.7 %collective-permute-done.21 = bf16[256,512]{1,0:T(8,128)(2,1)S(1)} collective-permute-done((bf16[256,512]{1,0:T(8,128)(2,1)S(1)}, bf16[256,512]{1,0:T(8,128)(2,1)S(1)}, u32[]{:S(2)}, u32[]{:S(2)}) %collective-permute-start.21) | collective-permute-done | bytes 262176 | tf_op jit(solution)/shard_map/ppermute | solution.py:13
  165.8 2.8 %collective-permute-start.22 = (bf16[256,512]{1,0:T(8,128)(2,1)S(1)}, bf16[256,512]{1,0:T(8,128)(2,1)S(1)}, u32[]{:S(2)}, u32[]{:S(2)}) collective-permute-start(bf16[256,512]{1,0:T(8,128)(2,1)S(1)} %get-tuple-element.31), channel_id=1, source_target_pairs={{0,128},{128,256},{256,384},{1,129},{129,257},{257,385},{2,130},{1... | collective-permute-start | bytes 786440 | tf_op jit(solution)/shard_map/ppermute | solution.py:13
  168.6 4.6 %collective-permute-done.22 = bf16[256,512]{1,0:T(8,128)(2,1)S(1)} collective-permute-done((bf16[256,512]{1,0:T(8,128)(2,1)S(1)}, bf16[256,512]{1,0:T(8,128)(2,1)S(1)}, u32[]{:S(2)}, u32[]{:S(2)}) %collective-permute-start.22) | collective-permute-done | bytes 262176 | tf_op jit(solution)/shard_map/ppermute | solution.py:13
  173.8 2.6 %collective-permute-start.23 = (bf16[256,512]{1,0:T(8,128)(2,1)S(1)}, bf16[256,512]{1,0:T(8,128)(2,1)S(1)}, u32[]{:S(2)}, u32[]{:S(2)}) collective-permute-start(bf16[256,512]{1,0:T(8,128)(2,1)S(1)} %bitcast.321), channel_id=1, source_target_pairs={{0,1},{1,2},{2,3},{3,4},{4,5},{5,6},{6,7},{7,8},{8,9},{9,10},{10,1... | collective-permute-start | bytes 786440 | tf_op jit(solution)/shard_map/ppermute | solution.py:13
  176.4 1.9 collective-permute-start.24
  178.3 2.8 %collective-permute-start.25 = (bf16[256,512]{1,0:T(8,128)(2,1)}, bf16[256,512]{1,0:T(8,128)(2,1)S(1)}, u32[]{:S(2)}, u32[]{:S(2)}) collective-permute-start(bf16[256,512]{1,0:T(8,128)(2,1)} %get-tuple-element.7), channel_id=1, source_target_pairs={{0,128},{128,256},{256,384},{1,129},{129,257},{257,385},{2,130},{1... | collective-permute-start | bytes 786440 | tf_op jit(solution)/shard_map/ppermute | solution.py:13
  181.2 6.2 %collective-permute-done.24 = bf16[256,512]{1,0:T(8,128)(2,1)S(1)} collective-permute-done((bf16[256,512]{1,0:T(8,128)(2,1)S(1)}, bf16[256,512]{1,0:T(8,128)(2,1)S(1)}, u32[]{:S(2)}, u32[]{:S(2)}) %collective-permute-start.24) | collective-permute-done | bytes 262176 | tf_op jit(solution)/shard_map/ppermute | solution.py:13
  190.7 4.1 %collective-permute-start.26 = (bf16[256,512]{1,0:T(8,128)(2,1)S(1)}, bf16[256,512]{1,0:T(8,128)(2,1)S(1)}, u32[]{:S(2)}, u32[]{:S(2)}) collective-permute-start(bf16[256,512]{1,0:T(8,128)(2,1)S(1)} %bitcast.309), channel_id=1, source_target_pairs={{0,1},{1,2},{2,3},{3,4},{4,5},{5,6},{6,7},{7,8},{8,9},{9,10},{10,1... | collective-permute-start | bytes 786440 | tf_op jit(solution)/shard_map/ppermute | solution.py:13
  194.8 1.9 collective-permute-start.27
  198.0 7.7 %collective-permute-done.27 = bf16[256,512]{1,0:T(8,128)(2,1)S(1)} collective-permute-done((bf16[256,512]{1,0:T(8,128)(2,1)S(1)}, bf16[256,512]{1,0:T(8,128)(2,1)S(1)}, u32[]{:S(2)}, u32[]{:S(2)}) %collective-permute-start.27) | collective-permute-done | bytes 262176 | tf_op jit(solution)/shard_map/ppermute | solution.py:13
  (152 shorter events, 34.7 us)
Async XLA Ops:
  0.0 18.7 %copy-start = (bf16[2,2,4,128,128]{4,3,2,1,0:T(8,128)(2,1)S(1)}, bf16[2,2,4,128,128]{4,3,2,1,0:T(8,128)(2,1)}, u32[]{:S(2)}) copy-start(bf16[2,2,4,128,128]{4,3,2,1,0:T(8,128)(2,1)} %param.11) | copy-start | bytes 1572868
  0.0 1.2 copy-start.6
  1.8 7.0 %copy-start.5 = (s32[2,2,4]{2,1,0:T(2,128)S(1)}, s32[2,2,4]{2,1,0:T(2,128)}, u32[]{:S(2)}) copy-start(s32[2,2,4]{2,1,0:T(2,128)} %param.13) | copy-start | bytes 196
  1.8 8.3 %collective-permute-start = (bf16[256,512]{1,0:T(8,128)(2,1)S(1)}, bf16[256,512]{1,0:T(8,128)(2,1)S(1)}, u32[]{:S(2)}, u32[]{:S(2)}) collective-permute-start(bf16[256,512]{1,0:T(8,128)(2,1)S(1)} %bitcast.303), channel_id=1, source_target_pairs={{0,1},{1,2},{2,3},{3,4},{4,5},{5,6},{6,7},{7,8},{8,9},{9,10},{10,1... | collective-permute-start | bytes 786440 | tf_op jit(solution)/shard_map/ppermute | solution.py:13
  6.8 11.0 %collective-permute-start.1 = (bf16[256,512]{1,0:T(8,128)(2,1)S(1)}, bf16[256,512]{1,0:T(8,128)(2,1)S(1)}, u32[]{:S(2)}, u32[]{:S(2)}) collective-permute-start(bf16[256,512]{1,0:T(8,128)(2,1)S(1)} %bitcast.304), channel_id=1, source_target_pairs={{1,0},{2,1},{3,2},{4,3},{5,4},{6,5},{7,6},{8,7},{9,8},{10,9},{11,1... | collective-permute-start | bytes 786440 | tf_op jit(solution)/shard_map/ppermute | solution.py:13
  18.7 1.2 copy-start.7
  20.8 5.2 %collective-permute-start.2 = (bf16[256,512]{1,0:T(8,128)(2,1)S(1)}, bf16[256,512]{1,0:T(8,128)(2,1)S(1)}, u32[]{:S(2)}, u32[]{:S(2)}) collective-permute-start(bf16[256,512]{1,0:T(8,128)(2,1)S(1)} %bitcast.305), channel_id=1, source_target_pairs={{0,1},{1,2},{2,3},{3,4},{4,5},{5,6},{6,7},{7,8},{8,9},{9,10},{10,1... | collective-permute-start | bytes 786440 | tf_op jit(solution)/shard_map/ppermute | solution.py:13
  22.7 11.0 %collective-permute-start.3 = (bf16[256,512]{1,0:T(8,128)(2,1)S(1)}, bf16[256,512]{1,0:T(8,128)(2,1)S(1)}, u32[]{:S(2)}, u32[]{:S(2)}) collective-permute-start(bf16[256,512]{1,0:T(8,128)(2,1)S(1)} %bitcast.306), channel_id=1, source_target_pairs={{1,0},{2,1},{3,2},{4,3},{5,4},{6,5},{7,6},{8,7},{9,8},{10,9},{11,1... | collective-permute-start | bytes 786440 | tf_op jit(solution)/shard_map/ppermute | solution.py:13
  34.9 1.2 copy-start.8
  36.1 9.4 %copy-start.3 = (bf16[128,512]{1,0:T(8,128)(2,1)S(1)}, bf16[128,512]{1,0:T(8,128)(2,1)}, u32[]{:S(2)}) copy-start(bf16[128,512]{1,0:T(8,128)(2,1)} %param.9) | copy-start | bytes 393220
  36.1 9.4 %copy-start.4 = (bf16[2,256,128]{2,1,0:T(8,128)(2,1)S(1)}, bf16[2,256,128]{2,1,0:T(8,128)(2,1)}, u32[]{:S(2)}) copy-start(bf16[2,256,128]{2,1,0:T(8,128)(2,1)} %param.8) | copy-start | bytes 393220
  36.5 9.1 %collective-permute-start.4 = (bf16[256,512]{1,0:T(8,128)(2,1)S(1)}, bf16[256,512]{1,0:T(8,128)(2,1)S(1)}, u32[]{:S(2)}, u32[]{:S(2)}) collective-permute-start(bf16[256,512]{1,0:T(8,128)(2,1)S(1)} %get-tuple-element.23), channel_id=1, source_target_pairs={{0,128},{128,256},{256,384},{1,129},{129,257},{257,385},{2,130},{1... | collective-permute-start | bytes 786440 | tf_op jit(solution)/shard_map/ppermute | solution.py:13
  39.6 20.9 %collective-permute-start.7 = (bf16[256,512]{1,0:T(8,128)(2,1)S(1)}, bf16[256,512]{1,0:T(8,128)(2,1)}, u32[]{:S(2)}, u32[]{:S(2)}) collective-permute-start(bf16[256,512]{1,0:T(8,128)(2,1)S(1)} %fusion.42), channel_id=1, source_target_pairs={{0,128},{128,256},{256,384},{1,129},{129,257},{257,385},{2,130},{1... | collective-permute-start | bytes 786440 | tf_op jit(solution)/shard_map/ppermute | solution.py:13
  46.3 5.2 %collective-permute-start.5 = (bf16[256,512]{1,0:T(8,128)(2,1)S(1)}, bf16[256,512]{1,0:T(8,128)(2,1)S(1)}, u32[]{:S(2)}, u32[]{:S(2)}) collective-permute-start(bf16[256,512]{1,0:T(8,128)(2,1)S(1)} %bitcast.311), channel_id=1, source_target_pairs={{0,1},{1,2},{2,3},{3,4},{4,5},{5,6},{6,7},{7,8},{8,9},{9,10},{10,1... | collective-permute-start | bytes 786440 | tf_op jit(solution)/shard_map/ppermute | solution.py:13
  48.2 11.0 %collective-permute-start.6 = (bf16[256,512]{1,0:T(8,128)(2,1)S(1)}, bf16[256,512]{1,0:T(8,128)(2,1)S(1)}, u32[]{:S(2)}, u32[]{:S(2)}) collective-permute-start(bf16[256,512]{1,0:T(8,128)(2,1)S(1)} %bitcast.312), channel_id=1, source_target_pairs={{1,0},{2,1},{3,2},{4,3},{5,4},{6,5},{7,6},{8,7},{9,8},{10,9},{11,1... | collective-permute-start | bytes 786440 | tf_op jit(solution)/shard_map/ppermute | solution.py:13
  60.5 1.3 copy-start.9
  62.6 5.2 %collective-permute-start.8 = (bf16[256,512]{1,0:T(8,128)(2,1)S(1)}, bf16[256,512]{1,0:T(8,128)(2,1)S(1)}, u32[]{:S(2)}, u32[]{:S(2)}) collective-permute-start(bf16[256,512]{1,0:T(8,128)(2,1)S(1)} %bitcast.313), channel_id=1, source_target_pairs={{0,1},{1,2},{2,3},{3,4},{4,5},{5,6},{6,7},{7,8},{8,9},{9,10},{10,1... | collective-permute-start | bytes 786440 | tf_op jit(solution)/shard_map/ppermute | solution.py:13
  64.5 11.0 %collective-permute-start.9 = (bf16[256,512]{1,0:T(8,128)(2,1)S(1)}, bf16[256,512]{1,0:T(8,128)(2,1)S(1)}, u32[]{:S(2)}, u32[]{:S(2)}) collective-permute-start(bf16[256,512]{1,0:T(8,128)(2,1)S(1)} %bitcast.314), channel_id=1, source_target_pairs={{1,0},{2,1},{3,2},{4,3},{5,4},{6,5},{7,6},{8,7},{9,8},{10,9},{11,1... | collective-permute-start | bytes 786440 | tf_op jit(solution)/shard_map/ppermute | solution.py:13
  76.4 1.2 copy-start.10
  76.8 1.0 copy-start.1
  78.1 7.1 %collective-permute-start.10 = (bf16[256,512]{1,0:T(8,128)(2,1)S(1)}, bf16[256,512]{1,0:T(8,128)(2,1)S(1)}, u32[]{:S(2)}, u32[]{:S(2)}) collective-permute-start(bf16[256,512]{1,0:T(8,128)(2,1)S(1)} %get-tuple-element.27), channel_id=1, source_target_pairs={{0,128},{128,256},{256,384},{1,129},{129,257},{257,385},{2,130},{1... | collective-permute-start | bytes 786440 | tf_op jit(solution)/shard_map/ppermute | solution.py:13
  85.8 7.7 %collective-permute-start.11 = (bf16[256,512]{1,0:T(8,128)(2,1)S(1)}, bf16[256,512]{1,0:T(8,128)(2,1)S(1)}, u32[]{:S(2)}, u32[]{:S(2)}) collective-permute-start(bf16[256,512]{1,0:T(8,128)(2,1)S(1)} %bitcast.315), channel_id=1, source_target_pairs={{0,1},{1,2},{2,3},{3,4},{4,5},{5,6},{6,7},{7,8},{8,9},{9,10},{10,1... | collective-permute-start | bytes 786440 | tf_op jit(solution)/shard_map/ppermute | solution.py:13
  88.7 11.0 %collective-permute-start.12 = (bf16[256,512]{1,0:T(8,128)(2,1)S(1)}, bf16[256,512]{1,0:T(8,128)(2,1)S(1)}, u32[]{:S(2)}, u32[]{:S(2)}) collective-permute-start(bf16[256,512]{1,0:T(8,128)(2,1)S(1)} %bitcast.316), channel_id=1, source_target_pairs={{1,0},{2,1},{3,2},{4,3},{5,4},{6,5},{7,6},{8,7},{9,8},{10,9},{11,1... | collective-permute-start | bytes 786440 | tf_op jit(solution)/shard_map/ppermute | solution.py:13
  90.7 10.3 %collective-permute-start.13 = (bf16[256,512]{1,0:T(8,128)(2,1)S(1)}, bf16[256,512]{1,0:T(8,128)(2,1)}, u32[]{:S(2)}, u32[]{:S(2)}) collective-permute-start(bf16[256,512]{1,0:T(8,128)(2,1)S(1)} %get-tuple-element.11), channel_id=1, source_target_pairs={{0,128},{128,256},{256,384},{1,129},{129,257},{257,385},{2,130},{1... | collective-permute-start | bytes 786440 | tf_op jit(solution)/shard_map/ppermute | solution.py:13
  100.9 1.3 copy-start.11
  103.1 8.2 %collective-permute-start.14 = (bf16[256,512]{1,0:T(8,128)(2,1)S(1)}, bf16[256,512]{1,0:T(8,128)(2,1)S(1)}, u32[]{:S(2)}, u32[]{:S(2)}) collective-permute-start(bf16[256,512]{1,0:T(8,128)(2,1)S(1)} %bitcast.317), channel_id=1, source_target_pairs={{0,1},{1,2},{2,3},{3,4},{4,5},{5,6},{6,7},{7,8},{8,9},{9,10},{10,1... | collective-permute-start | bytes 786440 | tf_op jit(solution)/shard_map/ppermute | solution.py:13
  108.0 11.0 %collective-permute-start.15 = (bf16[256,512]{1,0:T(8,128)(2,1)S(1)}, bf16[256,512]{1,0:T(8,128)(2,1)S(1)}, u32[]{:S(2)}, u32[]{:S(2)}) collective-permute-start(bf16[256,512]{1,0:T(8,128)(2,1)S(1)} %bitcast.318), channel_id=1, source_target_pairs={{1,0},{2,1},{3,2},{4,3},{5,4},{6,5},{7,6},{8,7},{9,8},{10,9},{11,1... | collective-permute-start | bytes 786440 | tf_op jit(solution)/shard_map/ppermute | solution.py:13
  119.9 1.2 copy-start.12
  120.2 1.0 copy-start.2
  121.6 7.4 %collective-permute-start.16 = (bf16[256,512]{1,0:T(8,128)(2,1)S(1)}, bf16[256,512]{1,0:T(8,128)(2,1)S(1)}, u32[]{:S(2)}, u32[]{:S(2)}) collective-permute-start(bf16[256,512]{1,0:T(8,128)(2,1)S(1)} %get-tuple-element.29), channel_id=1, source_target_pairs={{0,128},{128,256},{256,384},{1,129},{129,257},{257,385},{2,130},{1... | collective-permute-start | bytes 786440 | tf_op jit(solution)/shard_map/ppermute | solution.py:13
  129.5 7.6 %collective-permute-start.17 = (bf16[256,512]{1,0:T(8,128)(2,1)S(1)}, bf16[256,512]{1,0:T(8,128)(2,1)S(1)}, u32[]{:S(2)}, u32[]{:S(2)}) collective-permute-start(bf16[256,512]{1,0:T(8,128)(2,1)S(1)} %bitcast.307), channel_id=1, source_target_pairs={{0,1},{1,2},{2,3},{3,4},{4,5},{5,6},{6,7},{7,8},{8,9},{9,10},{10,1... | collective-permute-start | bytes 786440 | tf_op jit(solution)/shard_map/ppermute | solution.py:13
  132.1 11.0 %collective-permute-start.18 = (bf16[256,512]{1,0:T(8,128)(2,1)S(1)}, bf16[256,512]{1,0:T(8,128)(2,1)S(1)}, u32[]{:S(2)}, u32[]{:S(2)}) collective-permute-start(bf16[256,512]{1,0:T(8,128)(2,1)S(1)} %bitcast.308), channel_id=1, source_target_pairs={{1,0},{2,1},{3,2},{4,3},{5,4},{6,5},{7,6},{8,7},{9,8},{10,9},{11,1... | collective-permute-start | bytes 786440 | tf_op jit(solution)/shard_map/ppermute | solution.py:13
  134.2 10.2 %collective-permute-start.19 = (bf16[256,512]{1,0:T(8,128)(2,1)S(1)}, bf16[256,512]{1,0:T(8,128)(2,1)}, u32[]{:S(2)}, u32[]{:S(2)}) collective-permute-start(bf16[256,512]{1,0:T(8,128)(2,1)S(1)} %get-tuple-element.9), channel_id=1, source_target_pairs={{0,128},{128,256},{256,384},{1,129},{129,257},{257,385},{2,130},{1... | collective-permute-start | bytes 786440 | tf_op jit(solution)/shard_map/ppermute | solution.py:13
  144.4 1.9 copy-start.13
  147.1 8.4 %collective-permute-start.20 = (bf16[256,512]{1,0:T(8,128)(2,1)S(1)}, bf16[256,512]{1,0:T(8,128)(2,1)S(1)}, u32[]{:S(2)}, u32[]{:S(2)}) collective-permute-start(bf16[256,512]{1,0:T(8,128)(2,1)S(1)} %bitcast.319), channel_id=1, source_target_pairs={{0,1},{1,2},{2,3},{3,4},{4,5},{5,6},{6,7},{7,8},{8,9},{9,10},{10,1... | collective-permute-start | bytes 786440 | tf_op jit(solution)/shard_map/ppermute | solution.py:13
  152.1 11.0 %collective-permute-start.21 = (bf16[256,512]{1,0:T(8,128)(2,1)S(1)}, bf16[256,512]{1,0:T(8,128)(2,1)S(1)}, u32[]{:S(2)}, u32[]{:S(2)}) collective-permute-start(bf16[256,512]{1,0:T(8,128)(2,1)S(1)} %bitcast.320), channel_id=1, source_target_pairs={{1,0},{2,1},{3,2},{4,3},{5,4},{6,5},{7,6},{8,7},{9,8},{10,9},{11,1... | collective-permute-start | bytes 786440 | tf_op jit(solution)/shard_map/ppermute | solution.py:13
  164.0 1.4 copy-start.14
  165.8 7.4 %collective-permute-start.22 = (bf16[256,512]{1,0:T(8,128)(2,1)S(1)}, bf16[256,512]{1,0:T(8,128)(2,1)S(1)}, u32[]{:S(2)}, u32[]{:S(2)}) collective-permute-start(bf16[256,512]{1,0:T(8,128)(2,1)S(1)} %get-tuple-element.31), channel_id=1, source_target_pairs={{0,128},{128,256},{256,384},{1,129},{129,257},{257,385},{2,130},{1... | collective-permute-start | bytes 786440 | tf_op jit(solution)/shard_map/ppermute | solution.py:13
  173.8 7.4 %collective-permute-start.23 = (bf16[256,512]{1,0:T(8,128)(2,1)S(1)}, bf16[256,512]{1,0:T(8,128)(2,1)S(1)}, u32[]{:S(2)}, u32[]{:S(2)}) collective-permute-start(bf16[256,512]{1,0:T(8,128)(2,1)S(1)} %bitcast.321), channel_id=1, source_target_pairs={{0,1},{1,2},{2,3},{3,4},{4,5},{5,6},{6,7},{7,8},{8,9},{9,10},{10,1... | collective-permute-start | bytes 786440 | tf_op jit(solution)/shard_map/ppermute | solution.py:13
  176.4 11.0 %collective-permute-start.24 = (bf16[256,512]{1,0:T(8,128)(2,1)S(1)}, bf16[256,512]{1,0:T(8,128)(2,1)S(1)}, u32[]{:S(2)}, u32[]{:S(2)}) collective-permute-start(bf16[256,512]{1,0:T(8,128)(2,1)S(1)} %bitcast.322), channel_id=1, source_target_pairs={{1,0},{2,1},{3,2},{4,3},{5,4},{6,5},{7,6},{8,7},{9,8},{10,9},{11,1... | collective-permute-start | bytes 786440 | tf_op jit(solution)/shard_map/ppermute | solution.py:13
  178.3 10.3 %collective-permute-start.25 = (bf16[256,512]{1,0:T(8,128)(2,1)}, bf16[256,512]{1,0:T(8,128)(2,1)S(1)}, u32[]{:S(2)}, u32[]{:S(2)}) collective-permute-start(bf16[256,512]{1,0:T(8,128)(2,1)} %get-tuple-element.7), channel_id=1, source_target_pairs={{0,128},{128,256},{256,384},{1,129},{129,257},{257,385},{2,130},{1... | collective-permute-start | bytes 786440 | tf_op jit(solution)/shard_map/ppermute | solution.py:13
  188.6 1.2 copy-start.15
  190.7 7.4 %collective-permute-start.26 = (bf16[256,512]{1,0:T(8,128)(2,1)S(1)}, bf16[256,512]{1,0:T(8,128)(2,1)S(1)}, u32[]{:S(2)}, u32[]{:S(2)}) collective-permute-start(bf16[256,512]{1,0:T(8,128)(2,1)S(1)} %bitcast.309), channel_id=1, source_target_pairs={{0,1},{1,2},{2,3},{3,4},{4,5},{5,6},{6,7},{7,8},{8,9},{9,10},{10,1... | collective-permute-start | bytes 786440 | tf_op jit(solution)/shard_map/ppermute | solution.py:13
  194.8 11.0 %collective-permute-start.27 = (bf16[256,512]{1,0:T(8,128)(2,1)S(1)}, bf16[256,512]{1,0:T(8,128)(2,1)S(1)}, u32[]{:S(2)}, u32[]{:S(2)}) collective-permute-start(bf16[256,512]{1,0:T(8,128)(2,1)S(1)} %bitcast.310), channel_id=1, source_target_pairs={{1,0},{2,1},{3,2},{4,3},{5,4},{6,5},{7,6},{8,7},{9,8},{10,9},{11,1... | collective-permute-start | bytes 786440 | tf_op jit(solution)/shard_map/ppermute | solution.py:13
  207.0 1.2 copy-start.16
where the time goes:
time: 210 us; the launch traced here: 209 us
  waiting for transfers between devices  94.2 us (45%)
  starting transfers between devices  76.6 us (36%)
  local copies, waits for them, and re-layouts  15.4 us (7%)
  matrix products  13.3 us (6%)
  other arithmetic  8.5 us (4%)
    ppermute x28, waiting for transfers between devices, passed_along(): return lax.ppermute(block, axis, route)  94.2 us
    ppermute x28, starting transfers between devices, passed_along(): return lax.ppermute(block, axis, route)  76.6 us
    unnamed x35, local copies, waits for them, and re-layouts  7.01 us
    gather x10, local copies, waits for them, and re-layouts, shards(): jnp.take(table, sources.reshape(-1), axis=0)  6.14 us
    convert_element_type x10, other arithmetic, shards(): support = ((1.0 - residual_share) * aggregate + residual_share * initial....  5.81 us
    dot_general x10, matrix products, shards(): jnp.einsum('mn,nrd->mrd', select, blocks, preferred_element_type=jnp.floa...  4.86 us
  transfers between devices with their start and end apart: 28, of which 21 were waited for; matrix products, arithmetic and copies ran while one was open for 4% of the time, Pallas kernels for 0%

commit v1 on v0

v1 whole, which is shorter than its diff:
```python
import functools
import math

import jax
import jax.numpy as jnp
from jax import lax
from jax.experimental import pallas as pl
from jax.experimental.pallas import tpu as pltpu
from jax.sharding import PartitionSpec as P

MESH = pl.DeviceIdType.MESH
SHARE = 0.1
THETA = 0.5


def remote(src, dst, sent, landed, device):
    return pltpu.make_async_remote_copy(
        src_ref=src, dst_ref=dst, send_sem=sent, recv_sem=landed, device_id=device, device_id_type=MESH
    )


def kernel(
    sections, partitions, features, input_weight, weights, tiles, pub_ids, tile_src, out,
    table, last, slab, rows_in, proj, tile_buf, near_op, ghost_op, ints, support,
    local_sem, in_sent, feat_land, int_land, tile_land, near_sent, near_land, far_sent, far_land,
    slab_sent, slab_land, slab_pass, slab_swap, out_sent, out_land,
):
    block_total, tile_total = tiles.shape[1], tiles.shape[2]
    side = tiles.shape[3]
    rows = block_total * side
    half = weights.shape[1] // 2
    per_section = weights.shape[0]
    layers = sections * per_section
    final_section = sections - 1

    section = lax.axis_index("section")
    here = lax.axis_index("dom")
    core = lax.rem(here, 2)
    outward = 2 * core - 1
    wrap = lambda q: lax.rem(q + 2 * partitions, partitions)
    mate = wrap(here + outward)
    partner = wrap(here - outward)
    source = wrap(here + 2 * outward)
    target = wrap(here - 2 * outward)
    chain = (section == 0) | (section == final_section)
    group = jnp.where(section == 0, 1, 0)
    other_group = 1 - group
    at = lambda slot: pl.ds(slot * rows, rows)

    def local_half(layer, which):
        return (
            weights.at[layer - section * per_section, pl.ds(which * half, half)],
            slab.at[layer, pl.ds(which * half, half)],
        )

    feature_load = pltpu.make_async_copy(features.at[group], rows_in.at[at(2)], local_sem.at[0])
    tile_load = pltpu.make_async_copy(tiles.at[group], tile_buf.at[1], local_sem.at[1])
    proj_load = pltpu.make_async_copy(input_weight, proj, local_sem.at[2])

    @pl.when(chain)
    def _():
        feature_load.start()
        proj_load.start()
        tile_load.start()
        for i in range(per_section):
            layer = section * per_section + i
            src, dst = local_half(layer, core)
            pltpu.make_async_copy(src, dst, slab_land.at[layer]).start()
            src, dst = local_half(layer, 1 - core)
            pltpu.make_async_copy(src, dst, slab_swap.at[layer]).start()
        row = lax.broadcasted_iota(jnp.int32, (16, 128), 0)
        packed = jnp.zeros((16, 128), jnp.int32)
        for m in range(2):
            packed = jnp.where(row == m, pub_ids[group, m], packed)
        for b in range(block_total):
            for k in range(tile_total):
                packed = jnp.where(row == 2 + b * tile_total + k, tile_src[group, b, k], packed)
        ints[2] = packed

    barrier = pltpu.get_barrier_semaphore()
    peers = [(section, q) for q in (mate, partner, source, target)]
    peers += [(lax.rem(section + k, sections), here) for k in range(1, sections)]
    for peer in peers:
        pl.semaphore_signal(barrier, inc=1, device_id=peer, device_id_type=MESH)
    pl.semaphore_wait(barrier, len(peers))

    def slab_copy(i, which, plane):
        src = weights.at[i, pl.ds(core * half, half)]
        dst = slab.at[section * per_section + i, pl.ds(core * half, half)]
        landed = slab_land.at[section * per_section + i]
        return remote(src, dst, slab_sent.at[i, which], landed, (plane, here))

    def slab_sends(act):
        for i in range(per_section):
            for which, plane in enumerate((0, final_section)):
                @pl.when(section != plane)
                def _():
                    act(slab_copy(i, which, plane))

    def slab_forward(layer):
        part = slab.at[layer, pl.ds(core * half, half)]
        return remote(part, part, slab_pass.at[layer], slab_swap.at[layer], (section, partner))

    def near_copy(layer):
        return remote(
            table.at[layer, at(2)], table.at[layer, at(3)], near_sent.at[layer], near_land.at[layer],
            (section, partner),
        )

    def far_copy(layer):
        return remote(
            table.at[layer, at(2)], table.at[layer, at(0)], far_sent.at[layer], far_land.at[layer],
            (section, target),
        )

    def out_copy(state, plane):
        return remote(
            state, out.at[0, group], out_sent.at[plane], out_land.at[group], (plane, here)
        )

    def out_local(state):
        return pltpu.make_async_copy(state, out.at[0, group], local_sem.at[3])

    int_dests = ((0, target), (1, mate), (3, partner))

    def int_copy(n):
        slot, q = int_dests[n]
        return remote(ints.at[2], ints.at[slot], in_sent.at[n], int_land.at[slot], (section, q))

    def feature_copy(n):
        slot, q = int_dests[n]
        return remote(
            features.at[group], rows_in.at[at(slot)], in_sent.at[3 + n], feat_land.at[slot], (section, q)
        )

    tile_copy = remote(tiles.at[group], tile_buf.at[0], in_sent.at[6], tile_land.at[0], (section, mate))

    @pl.when(chain)
    def _():
        for n in (1, 2, 0):
            feature_copy(n).start()
        for n in range(3):
            int_copy(n).start()
        tile_copy.start()

    slab_sends(lambda copy: copy.start())

    def build(op, tile_slot, int_slot, outer, inner):
        outer_pub = [ints[outer, m : m + 1, :] for m in range(2)]
        inner_pub = [ints[inner, m : m + 1, :] for m in range(2)]
        before = [jnp.where(core == 0, a, 4 + b) for a, b in zip(outer_pub, inner_pub)]
        after = [jnp.where(core == 0, 4 + b, a) for a, b in zip(outer_pub, inner_pub)]
        for b in range(block_total):
            columns = []
            for k in range(tile_total):
                n = 2 + b * tile_total + k
                slot = ints[int_slot, n : n + 1, :]
                column = jnp.where(slot < 2, 2 + slot, after[1])
                column = jnp.where(slot == 2, before[0], column)
                column = jnp.where(slot == 3, before[1], column)
                column = jnp.where(slot == 4, after[0], column)
                columns.append(column)
            pieces = [tile_buf[tile_slot, b, k].astype(jnp.float32) for k in range(tile_total)]
            for j in range(6):
                total = jnp.zeros((side, side), jnp.float32)
                for k in range(tile_total):
                    total += pieces[k] * (columns[k] == j).astype(jnp.float32)
                op[b * side : (b + 1) * side, j * side : (j + 1) * side] = total.astype(jnp.bfloat16)

    def propagate(op, layer, base, dst):
        beta = jnp.float32(0.0)
        for i in range(layers):
            beta = jnp.where(layer == i, jnp.float32(math.log(THETA / (i + 1) + 1.0)), beta)
        aggregate = jnp.dot(
            op[...], table[layer, base * rows : (base + 3) * rows, :], preferred_element_type=jnp.float32
        )
        initial = table[0, (base + 1) * rows : (base + 2) * rows, :].astype(jnp.float32)
        support[...] = ((1.0 - SHARE) * aggregate + SHARE * initial).astype(jnp.bfloat16)
        product = jnp.dot(support[...], slab[layer], preferred_element_type=jnp.float32)
        mixed = (1.0 - beta) * support[...].astype(jnp.float32) + beta * product
        dst[...] = jnp.maximum(mixed, 0.0).astype(jnp.bfloat16)

    def slab_ready(layer):
        slab_forward_half = slab.at[layer, pl.ds(core * half, half)]
        pltpu.make_async_copy(slab_forward_half, slab_forward_half, slab_land.at[layer]).wait()

        @pl.when(layer // per_section != section)
        def _():
            slab_forward(layer).start()

    def slab_swapped(layer):
        part = slab.at[layer, pl.ds((1 - core) * half, half)]
        pltpu.make_async_copy(part, part, slab_swap.at[layer]).wait()

    @pl.when(chain)
    def _():
        feature_load.wait()
        proj_load.wait()
        for n in (2, 1, 0):
            feature_copy(n).wait_recv()
        table[0] = jnp.maximum(
            jnp.dot(rows_in[...], proj[...], preferred_element_type=jnp.float32), 0.0
        ).astype(jnp.bfloat16)
        tile_load.wait()
        for n in range(3):
            int_copy(n).wait_recv()
        build(near_op, 1, 2, 1, 3)
        slab_ready(0)

        def step(layer, carry):
            slab_swapped(layer)

            @pl.when(layer > 0)
            def _():
                near_copy(layer).wait_recv()

            propagate(near_op, layer, 1, table.at[layer + 1, at(2)])
            near_copy(layer + 1).start()

            @pl.when(layer < layers - 2)
            def _():
                far_copy(layer + 1).start()

            @pl.when(lax.rem(layer + 1, per_section) == 0)
            def _():
                plane = (layer + 1) // per_section - 1
                state = table.at[layer + 1, at(2)]

                @pl.when(plane == section)
                def _():
                    out_local(state).start()

                @pl.when(plane != section)
                def _():
                    out_copy(state, plane).start()

            slab_ready(layer + 1)

            @pl.when(layer == 0)
            def _():
                tile_copy.wait_recv()
                build(ghost_op, 0, 1, 0, 2)

            @pl.when(layer > 0)
            def _():
                far_copy(layer).wait_recv()

            propagate(ghost_op, layer, 0, table.at[layer + 1, at(1)])
            return carry

        lax.fori_loop(0, layers - 1, step, 0)
        end = layers - 1
        slab_swapped(end)
        near_copy(end).wait_recv()
        propagate(near_op, end, 1, last)

        @pl.when(section == final_section)
        def _():
            out_local(last).start()

        @pl.when(section != final_section)
        def _():
            out_copy(last, final_section).start()

        for n in range(3):
            int_copy(n).wait_send()
            feature_copy(n).wait_send()
        tile_copy.wait_send()
        for layer in range(1, layers):
            near_copy(layer).wait_send()
            if layer < layers - 1:
                far_copy(layer).wait_send()
        for layer in range(layers):
            @pl.when(layer // per_section != section)
            def _():
                slab_forward(layer).wait_send()
        for plane in range(sections):
            @pl.when(plane != section)
            def _():
                out_copy(last, plane).wait_send()
        out_local(last).wait()

        arriving = out.at[0, other_group]
        pltpu.make_async_copy(arriving, arriving, out_land.at[other_group]).wait()

    @pl.when(jnp.logical_not(chain))
    def _():
        for g in range(2):
            pltpu.make_async_copy(out.at[0, g], out.at[0, g], out_land.at[g]).wait()

    slab_sends(lambda copy: copy.wait_send())


def shards(features, input_weight, layer_weights, tiles, pub_ids, tile_src):
    groups, rows, width_in = features.shape
    width = input_weight.shape[1]
    block_total, tile_total, side = tiles.shape[1:4]
    per_section = layer_weights.shape[0]
    sections = lax.axis_size("section")
    partitions = lax.axis_size("dom")
    layers = sections * per_section
    anywhere = pl.BlockSpec(memory_space=pl.ANY)
    scalars = pl.BlockSpec(memory_space=pltpu.SMEM)
    dma = pltpu.SemaphoreType.DMA
    bf16 = jnp.bfloat16
    return pl.pallas_call(
        functools.partial(kernel, sections, partitions),
        out_shape=jax.ShapeDtypeStruct((1, groups, rows, width), bf16),
        in_specs=[anywhere] * 4 + [scalars] * 2,
        out_specs=anywhere,
        scratch_shapes=[
            pltpu.VMEM((layers, 4 * rows, width), bf16),
            pltpu.VMEM((rows, width), bf16),
            pltpu.VMEM((layers, width, width), bf16),
            pltpu.VMEM((4 * rows, width_in), bf16),
            pltpu.VMEM((width_in, width), bf16),
            pltpu.VMEM((2, block_total, tile_total, side, side), bf16),
            pltpu.VMEM((rows, 3 * rows), bf16),
            pltpu.VMEM((rows, 3 * rows), bf16),
            pltpu.VMEM((4, 16, 128), jnp.int32),
            pltpu.VMEM((rows, width), bf16),
            dma((4,)),
            dma((7,)),
            dma((4,)),
            dma((4,)),
            dma((1,)),
            dma((layers,)),
            dma((layers,)),
            dma((layers,)),
            dma((layers,)),
            dma((per_section, 2)),
            dma((layers,)),
            dma((layers,)),
            dma((layers,)),
            dma((sections,)),
            dma((groups,)),
        ],
        compiler_params=pltpu.CompilerParams(collective_id=0, has_side_effects=True),
    )(features, input_weight, layer_weights, tiles, pub_ids, tile_src)


def solution(mesh):
    in_specs = (
        P(None, "dom", None),
        P(),
        P("section", None, None),
        P(None, "dom", None, None, None),
        P(None, "dom"),
        P(None, "dom", None),
    )
    out_specs = P("section", None, "dom", None)
    return jax.shard_map(shards, mesh=mesh, in_specs=in_specs, out_specs=out_specs, check_vma=False)
```

time: 210 us -> 59.8 us (0.28)
  the two profiles are of different devices: /device:TPU:251 before, /device:TPU:6 now
where the time goes in v1:
time: 59.8 us; the launch traced here: 59.6 us
  Pallas kernels  57.7 us (96%)
  local copies, waits for them, and re-layouts  1.87 us (3%)
    pallas_call x1, Pallas kernels, shards(): pl.pallas_call(functools.partial(kernel, sections, partitions), out_shape...  57.7 us
    unnamed x1, local copies, waits for them, and re-layouts  1.87 us

profile of v1, /device:TPU:6, one launch (start us, length us, event | category | flops | bytes accessed | tf_op | source)
XLA Modules:
  0.0 59.6 jit_solution(12336390451056982076)
XLA Ops:
  0.0 57.7 %shard_map.64 = bf16[1,2,256,512]{3,2,1,0:T(8,128)(2,1)} custom-call(bf16[2,256,128]{2,1,0:T(8,128)(2,1)} %features.1, bf16[128,512]{1,0:T(8,128)(2,1)} %input_weight.1, bf16[2,512,512]{2,1,0:T(8,128)(2,1)} %weights.1, bf16[2,2,4,128,128]{4,3,2,1,0:T(8,128)(2,1)} %tiles.1, s32[2,2]{1,0:T(2,128)} %pub_ids.1, s32[2,2,4]{2,1,0:T(2,128)} %tile_src.1), custom_call_target="tpu_custom_call" | custom-call | tf_op jit(solution)/shard_map/pallas_call | solution.py:306
  57.7 1.9 %copy.8 = bf16[1,2,256,512]{3,2,1,0:T(8,128)(2,1)} copy(bf16[1,2,256,512]{3,2,1,0:T(8,128)(2,1)} %shard_map.64) | data formatting | bytes 1048576

commit v2 on v1

--- a/solution.py
+++ b/solution.py
@@ -21,7 +21,7 @@
 
 def kernel(
     sections, partitions, features, input_weight, weights, tiles, pub_ids, tile_src, out,
-    table, last, slab, rows_in, proj, tile_buf, near_op, ghost_op, ints, support,
+    table, last, slab, rows_in, proj, tile_buf, near_op, ghost_op, ints, support, near_sum, ghost_sum,
     local_sem, in_sent, feat_land, int_land, tile_land, near_sent, near_land, far_sent, far_land,
     slab_sent, slab_land, slab_pass, slab_swap, out_sent, out_land,
 ):
@@ -45,6 +45,9 @@
     chain = (section == 0) | (section == final_section)
     group = jnp.where(section == 0, 1, 0)
     other_group = 1 - group
+    inner = (here != 0) & (here != partitions - 1)
+    to_target = (target != 0) & (target != partitions - 1)
+    piece = rows // 2
     at = lambda slot: pl.ds(slot * rows, rows)
 
     def local_half(layer, which):
@@ -84,42 +87,52 @@
         pl.semaphore_signal(barrier, inc=1, device_id=peer, device_id_type=MESH)
     pl.semaphore_wait(barrier, len(peers))
 
-    def slab_copy(i, which, plane):
-        src = weights.at[i, pl.ds(core * half, half)]
-        dst = slab.at[section * per_section + i, pl.ds(core * half, half)]
-        landed = slab_land.at[section * per_section + i]
-        return remote(src, dst, slab_sent.at[i, which], landed, (plane, here))
-
-    def slab_sends(act):
-        for i in range(per_section):
-            for which, plane in enumerate((0, final_section)):
-                @pl.when(section != plane)
-                def _():
-                    act(slab_copy(i, which, plane))
+    def slab_copy(n, layer, plane):
+        part = pl.ds(core * half, half)
+        if layer // per_section == plane_of[n]:
+            src = weights.at[layer % per_section, part]
+        else:
+            src = slab.at[layer, part]
+        return remote(src, slab.at[layer, part], slab_sent.at[n % 5], slab_land.at[layer], (plane, here))
+
+    plane_of = [0] * 5 + [1] * 5 + [2] * 5 + [3] * 5
+    routes = {
+        0: ((0, 3), (1, 3)),
+        1: ((2, 0), (2, 2), (3, 0), (3, 3), (5, 0)),
+        2: ((4, 0), (5, 1), (2, 3), (4, 3), (5, 3)),
+        3: ((6, 0), (7, 0)),
+    }
+
+    def slab_sends(plane):
+        return [slab_copy(5 * plane + n, layer, to) for n, (layer, to) in enumerate(routes[plane])]
 
     def slab_forward(layer):
         part = slab.at[layer, pl.ds(core * half, half)]
         return remote(part, part, slab_pass.at[layer], slab_swap.at[layer], (section, partner))
 
-    def near_copy(layer):
+    def near_copy(layer, m=None):
+        src, dst = (at(2), at(3)) if m is None else (pl.ds(2 * rows + m * piece, piece), pl.ds(3 * rows + m * piece, piece))
         return remote(
-            table.at[layer, at(2)], table.at[layer, at(3)], near_sent.at[layer], near_land.at[layer],
+            table.at[layer, src], table.at[layer, dst], near_sent.at[layer], near_land.at[layer],
             (section, partner),
         )
 
-    def far_copy(layer):
+    def far_copy(layer, m=None):
+        src, dst = (at(2), at(0)) if m is None else (pl.ds(2 * rows + m * piece, piece), pl.ds(m * piece, piece))
         return remote(
-            table.at[layer, at(2)], table.at[layer, at(0)], far_sent.at[layer], far_land.at[layer],
+            table.at[layer, src], table.at[layer, dst], far_sent.at[layer], far_land.at[layer],
             (section, target),
         )
 
-    def out_copy(state, plane):
+    def out_copy(state, plane, m=None):
+        part = pl.ds(0, rows) if m is None else pl.ds(m * piece, piece)
         return remote(
-            state, out.at[0, group], out_sent.at[plane], out_land.at[group], (plane, here)
-        )
-
-    def out_local(state):
-        return pltpu.make_async_copy(state, out.at[0, group], local_sem.at[3])
+            state, out.at[0, group, part], out_sent.at[plane], out_land.at[group], (plane, here)
+        )
+
+    def out_local(state, m=None):
+        part = pl.ds(0, rows) if m is None else pl.ds(m * piece, piece)
+        return pltpu.make_async_copy(state, out.at[0, group, part], local_sem.at[3])
 
     int_dests = ((0, target), (1, mate), (3, partner))
 
@@ -135,15 +148,28 @@
 
     tile_copy = remote(tiles.at[group], tile_buf.at[0], in_sent.at[6], tile_land.at[0], (section, mate))
 
+    takes = (inner, inner, None)
+    gives = (to_target, inner, None)
+
+    def each(flags, n, act):
+        if flags[n] is None:
+            act()
+        else:
+            pl.when(flags[n])(act)
+
     @pl.when(chain)
     def _():
         for n in (1, 2, 0):
-            feature_copy(n).start()
-        for n in range(3):
-            int_copy(n).start()
-        tile_copy.start()
-
-    slab_sends(lambda copy: copy.start())
+            each(gives, n, lambda: int_copy(n).start())
+        for n in (1, 2, 0):
+            each(gives, n, lambda: feature_copy(n).start())
+        each(gives, 1, lambda: tile_copy.start())
+
+    for plane in (0, 3):
+        @pl.when(section == plane)
+        def _():
+            for copy in slab_sends(plane):
+                copy.start()
 
     def build(op, tile_slot, int_slot, outer, inner):
         outer_pub = [ints[outer, m : m + 1, :] for m in range(2)]
@@ -167,18 +193,28 @@
                     total += pieces[k] * (columns[k] == j).astype(jnp.float32)
                 op[b * side : (b + 1) * side, j * side : (j + 1) * side] = total.astype(jnp.bfloat16)
 
-    def propagate(op, layer, base, dst):
+    def gather(op, layer, base, total):
+        total[...] = jnp.dot(
+            op[:, rows:], table[layer, (base + 1) * rows : (base + 3) * rows, :], preferred_element_type=jnp.float32
+        )
+
+    def propagate(op, layer, base, total, dst, done):
         beta = jnp.float32(0.0)
         for i in range(layers):
             beta = jnp.where(layer == i, jnp.float32(math.log(THETA / (i + 1) + 1.0)), beta)
-        aggregate = jnp.dot(
-            op[...], table[layer, base * rows : (base + 3) * rows, :], preferred_element_type=jnp.float32
-        )
-        initial = table[0, (base + 1) * rows : (base + 2) * rows, :].astype(jnp.float32)
-        support[...] = ((1.0 - SHARE) * aggregate + SHARE * initial).astype(jnp.bfloat16)
-        product = jnp.dot(support[...], slab[layer], preferred_element_type=jnp.float32)
-        mixed = (1.0 - beta) * support[...].astype(jnp.float32) + beta * product
-        dst[...] = jnp.maximum(mixed, 0.0).astype(jnp.bfloat16)
+        for m in range(2):
+            part = slice(m * piece, (m + 1) * piece)
+            aggregate = total[part, :] + jnp.dot(
+                op[part, :rows], table[layer, base * rows : (base + 1) * rows, :], preferred_element_type=jnp.float32
+            )
+            start = (base + 1) * rows + m * piece
+            initial = table[0, start : start + piece, :].astype(jnp.float32)
+            mixed = ((1.0 - SHARE) * aggregate + SHARE * initial).astype(jnp.bfloat16)
+            support[part, :] = mixed
+            product = jnp.dot(support[part, :], slab[layer], preferred_element_type=jnp.float32)
+            state = (1.0 - beta) * support[part, :].astype(jnp.float32) + beta * product
+            dst[part, :] = jnp.maximum(state, 0.0).astype(jnp.bfloat16)
+            done(m)
 
     def slab_ready(layer):
         slab_forward_half = slab.at[layer, pl.ds(core * half, half)]
@@ -192,34 +228,44 @@
         part = slab.at[layer, pl.ds((1 - core) * half, half)]
         pltpu.make_async_copy(part, part, slab_swap.at[layer]).wait()
 
+    def project(first, last_slot):
+        part = slice(first * rows, last_slot * rows)
+        table[0, part, :] = jnp.maximum(
+            jnp.dot(rows_in[part, :], proj[...], preferred_element_type=jnp.float32), 0.0
+        ).astype(jnp.bfloat16)
+
     @pl.when(chain)
     def _():
+        @pl.when(jnp.logical_not(inner))
+        def _():
+            for layer in range(1, layers):
+                table[layer, at(1)] = jnp.zeros((rows, table.shape[2]), jnp.bfloat16)
+            rows_in[0 : 2 * rows, :] = jnp.zeros((2 * rows, rows_in.shape[1]), jnp.bfloat16)
+            ints[0:2] = jnp.zeros((2, 16, 128), jnp.int32)
+
+        tile_load.wait()
+        for n in (1, 2, 0):
+            each(takes, n, lambda: int_copy(n).wait_recv())
+        build(near_op, 1, 2, 1, 3)
         feature_load.wait()
         proj_load.wait()
-        for n in (2, 1, 0):
-            feature_copy(n).wait_recv()
-        table[0] = jnp.maximum(
-            jnp.dot(rows_in[...], proj[...], preferred_element_type=jnp.float32), 0.0
-        ).astype(jnp.bfloat16)
-        tile_load.wait()
-        for n in range(3):
-            int_copy(n).wait_recv()
-        build(near_op, 1, 2, 1, 3)
+        for n in (2, 1):
+            each(takes, n, lambda: feature_copy(n).wait_recv())
+        project(1, 4)
+        gather(near_op, 0, 1, near_sum)
         slab_ready(0)
 
         def step(layer, carry):
             slab_swapped(layer)
 
-            @pl.when(layer > 0)
-            def _():
-                near_copy(layer).wait_recv()
-
-            propagate(near_op, layer, 1, table.at[layer + 1, at(2)])
-            near_copy(layer + 1).start()
-
-            @pl.when(layer < layers - 2)
-            def _():
-                far_copy(layer + 1).start()
+            def send(m):
+                near_copy(layer + 1, m).start()
+
+                @pl.when((layer < layers - 2) & to_target)
+                def _():
+                    far_copy(layer + 1, m).start()
+
+            propagate(near_op, layer, 1, near_sum, table.at[layer + 1, at(2)], send)
 
             @pl.when(lax.rem(layer + 1, per_section) == 0)
             def _():
@@ -236,40 +282,57 @@
 
             slab_ready(layer + 1)
 
-            @pl.when(layer == 0)
-            def _():
+            @pl.when((layer == 0) & inner)
+            def _():
+                feature_copy(0).wait_recv()
+                project(0, 1)
                 tile_copy.wait_recv()
                 build(ghost_op, 0, 1, 0, 2)
 
-            @pl.when(layer > 0)
+            @pl.when(inner)
+            def _():
+                gather(ghost_op, layer, 0, ghost_sum)
+
+            near_copy(layer + 1).wait_recv()
+            gather(near_op, layer + 1, 1, near_sum)
+
+            @pl.when((layer > 0) & inner)
             def _():
                 far_copy(layer).wait_recv()
 
-            propagate(ghost_op, layer, 0, table.at[layer + 1, at(1)])
+            @pl.when(inner)
+            def _():
+                propagate(ghost_op, layer, 0, ghost_sum, table.at[layer + 1, at(1)], lambda m: None)
+
             return carry
 
         lax.fori_loop(0, layers - 1, step, 0)
         end = layers - 1
         slab_swapped(end)
-        near_copy(end).wait_recv()
-        propagate(near_op, end, 1, last)
-
-        @pl.when(section == final_section)
-        def _():
-            out_local(last).start()
-
-        @pl.when(section != final_section)
-        def _():
-            out_copy(last, final_section).start()
+
+        def finish(m):
+            state = last.at[pl.ds(m * piece, piece)]
+
+            @pl.when(section == final_section)
+            def _():
+                out_local(state, m).start()
+
+            @pl.when(section != final_section)
+            def _():
+                out_copy(state, final_section, m).start()
+
+        propagate(near_op, end, 1, near_sum, last, finish)
 
         for n in range(3):
-            int_copy(n).wait_send()
-            feature_copy(n).wait_send()
-        tile_copy.wait_send()
+            each(gives, n, lambda: int_copy(n).wait_send())
+            each(gives, n, lambda: feature_copy(n).wait_send())
+        each(gives, 1, lambda: tile_copy.wait_send())
         for layer in range(1, layers):
             near_copy(layer).wait_send()
             if layer < layers - 1:
-                far_copy(layer).wait_send()
+                @pl.when(to_target)
+                def _():
+                    far_copy(layer).wait_send()
         for layer in range(layers):
             @pl.when(layer // per_section != section)
             def _():
@@ -279,16 +342,31 @@
             def _():
                 out_copy(last, plane).wait_send()
         out_local(last).wait()
+        for plane in (0, 3):
+            @pl.when(section == plane)
+            def _():
+                for copy in slab_sends(plane):
+                    copy.wait_send()
 
         arriving = out.at[0, other_group]
         pltpu.make_async_copy(arriving, arriving, out_land.at[other_group]).wait()
 
-    @pl.when(jnp.logical_not(chain))
-    def _():
-        for g in range(2):
-            pltpu.make_async_copy(out.at[0, g], out.at[0, g], out_land.at[g]).wait()
-
-    slab_sends(lambda copy: copy.wait_send())
+    def slab_arrived(layer):
+        part = slab.at[layer, pl.ds(core * half, half)]
+        pltpu.make_async_copy(part, part, slab_land.at[layer]).wait()
+
+    for plane, relayed in ((1, 5), (2, 2)):
+        @pl.when(section == plane)
+        def _():
+            copies = slab_sends(plane)
+            for (layer, to), copy in zip(routes[plane], copies):
+                if layer == relayed:
+                    slab_arrived(layer)
+                copy.start()
+            for copy in copies:
+                copy.wait_send()
+            for g in range(2):
+                pltpu.make_async_copy(out.at[0, g], out.at[0, g], out_land.at[g]).wait()
 
 
 def shards(features, input_weight, layer_weights, tiles, pub_ids, tile_src):
@@ -319,6 +397,8 @@
             pltpu.VMEM((rows, 3 * rows), bf16),
             pltpu.VMEM((4, 16, 128), jnp.int32),
             pltpu.VMEM((rows, width), bf16),
+            pltpu.VMEM((rows, width), jnp.float32),
+            pltpu.VMEM((rows, width), jnp.float32),
             dma((4,)),
             dma((7,)),
             dma((4,)),
@@ -328,7 +408,7 @@
             dma((layers,)),
             dma((layers,)),
             dma((layers,)),
-            dma((per_section, 2)),
+            dma((5,)),
             dma((layers,)),
             dma((layers,)),
             dma((layers,)),

time: 59.8 us -> 54.5 us (0.911)
  the two profiles are of different devices: /device:TPU:6 before, /device:TPU:1 now
where the time goes in v2:
time: 54.5 us; the launch traced here: 54.4 us
  Pallas kernels  52.5 us (96%)
  local copies, waits for them, and re-layouts  1.87 us (3%)
    pallas_call x1, Pallas kernels, shards(): pl.pallas_call(functools.partial(kernel, sections, partitions), out_shape...  52.5 us
    unnamed x1, local copies, waits for them, and re-layouts  1.87 us

profile of v2, /device:TPU:1, one launch (start us, length us, event | category | flops | bytes accessed | tf_op | source)
XLA Modules:
  0.0 54.4 jit_solution(9935009493056326518)
XLA Ops:
  0.0 52.5 %shard_map.64 = bf16[1,2,256,512]{3,2,1,0:T(8,128)(2,1)} custom-call(bf16[2,256,128]{2,1,0:T(8,128)(2,1)} %features.1, bf16[128,512]{1,0:T(8,128)(2,1)} %input_weight.1, bf16[2,512,512]{2,1,0:T(8,128)(2,1)} %weights.1, bf16[2,2,4,128,128]{4,3,2,1,0:T(8,128)(2,1)} %tiles.1, s32[2,2]{1,0:T(2,128)} %pub_ids.1, s32[2,2,4]{2,1,0:T(2,128)} %tile_src.1), custom_call_target="tpu_custom_call" | custom-call | tf_op jit(solution)/shard_map/pallas_call | solution.py:384
  52.5 1.9 %copy.8 = bf16[1,2,256,512]{3,2,1,0:T(8,128)(2,1)} copy(bf16[1,2,256,512]{3,2,1,0:T(8,128)(2,1)} %shard_map.64) | data formatting | bytes 1048576

commit v3 on v2

--- a/solution.py
+++ b/solution.py
@@ -81,11 +81,23 @@
         ints[2] = packed
 
     barrier = pltpu.get_barrier_semaphore()
-    peers = [(section, q) for q in (mate, partner, source, target)]
-    peers += [(lax.rem(section + k, sections), here) for k in range(1, sections)]
-    for peer in peers:
-        pl.semaphore_signal(barrier, inc=1, device_id=peer, device_id_type=MESH)
-    pl.semaphore_wait(barrier, len(peers))
+    def greet(device):
+        pl.semaphore_signal(barrier, inc=1, device_id=device, device_id_type=MESH)
+
+    greet((section, partner))
+    for k in range(1, sections):
+        greet((lax.rem(section + k, sections), here))
+
+    @pl.when(inner)
+    def _():
+        greet((section, mate))
+        greet((section, source))
+
+    @pl.when(to_target)
+    def _():
+        greet((section, target))
+
+    pl.semaphore_wait(barrier, sections + 2 * inner.astype(jnp.int32) + to_target.astype(jnp.int32))
 
     def slab_copy(n, layer, plane):
         part = pl.ds(core * half, half)

time: 54.5 us -> 49.6 us (0.910)
  the two profiles are of different devices: /device:TPU:1 before, /device:TPU:5 now
where the time goes in v3:
time: 49.6 us; the launch traced here: 49.4 us
  Pallas kernels  47.5 us (96%)
  local copies, waits for them, and re-layouts  1.87 us (4%)
    pallas_call x1, Pallas kernels, shards(): pl.pallas_call(functools.partial(kernel, sections, partitions), out_shape...  47.5 us
    unnamed x1, local copies, waits for them, and re-layouts  1.87 us

profile of v3, /device:TPU:5, one launch (start us, length us, event | category | flops | bytes accessed | tf_op | source)
XLA Modules:
  0.0 49.4 jit_solution(1475694891784254465)
XLA Ops:
  0.0 47.5 %shard_map.64 = bf16[1,2,256,512]{3,2,1,0:T(8,128)(2,1)} custom-call(bf16[2,256,128]{2,1,0:T(8,128)(2,1)} %features.1, bf16[128,512]{1,0:T(8,128)(2,1)} %input_weight.1, bf16[2,512,512]{2,1,0:T(8,128)(2,1)} %weights.1, bf16[2,2,4,128,128]{4,3,2,1,0:T(8,128)(2,1)} %tiles.1, s32[2,2]{1,0:T(2,128)} %pub_ids.1, s32[2,2,4]{2,1,0:T(2,128)} %tile_src.1), custom_call_target="tpu_custom_call" | custom-call | tf_op jit(solution)/shard_map/pallas_call | solution.py:396
  47.5 1.9 %copy.8 = bf16[1,2,256,512]{3,2,1,0:T(8,128)(2,1)} copy(bf16[1,2,256,512]{3,2,1,0:T(8,128)(2,1)} %shard_map.64) | data formatting | bytes 1048576

commit v4 on v3

--- a/solution.py
+++ b/solution.py
@@ -110,8 +110,8 @@
     plane_of = [0] * 5 + [1] * 5 + [2] * 5 + [3] * 5
     routes = {
         0: ((0, 3), (1, 3)),
-        1: ((2, 0), (2, 2), (3, 0), (3, 3), (5, 0)),
-        2: ((4, 0), (5, 1), (2, 3), (4, 3), (5, 3)),
+        1: ((2, 0), (2, 2), (3, 0), (3, 2), (5, 0)),
+        2: ((5, 1), (4, 0), (2, 3), (3, 3), (5, 3)),
         3: ((6, 0), (7, 0)),
     }
 
@@ -236,6 +236,10 @@
         def _():
             slab_forward(layer).start()
 
+        @pl.when((layer == 4) & (section == 0))
+        def _():
+            slab_copy(4, 4, 3).start()
+
     def slab_swapped(layer):
         part = slab.at[layer, pl.ds((1 - core) * half, half)]
         pltpu.make_async_copy(part, part, slab_swap.at[layer]).wait()
@@ -360,6 +364,10 @@
                 for copy in slab_sends(plane):
                     copy.wait_send()
 
+        @pl.when(section == 0)
+        def _():
+            slab_copy(4, 4, 3).wait_send()
+
         arriving = out.at[0, other_group]
         pltpu.make_async_copy(arriving, arriving, out_land.at[other_group]).wait()
 
@@ -367,12 +375,12 @@
         part = slab.at[layer, pl.ds(core * half, half)]
         pltpu.make_async_copy(part, part, slab_land.at[layer]).wait()
 
-    for plane, relayed in ((1, 5), (2, 2)):
+    for plane in (1, 2):
         @pl.when(section == plane)
         def _():
             copies = slab_sends(plane)
             for (layer, to), copy in zip(routes[plane], copies):
-                if layer == relayed:
+                if layer // per_section != plane:
                     slab_arrived(layer)
                 copy.start()
             for copy in copies:

time: 49.6 us -> 45.7 us (0.921)
  Pallas kernels: 47.5 us -> 43.6 us
    pallas_call x1, Pallas kernels: 47.5 us -> 43.6 us  [shards(): pl.pallas_call(functools.partial(kernel, sections, partitions), out_shape...]
where the time goes in v4:
time: 45.7 us; the launch traced here: 45.5 us
  Pallas kernels  43.6 us (95%)
  local copies, waits for them, and re-layouts  1.87 us (4%)
    pallas_call x1, Pallas kernels, shards(): pl.pallas_call(functools.partial(kernel, sections, partitions), out_shape...  43.6 us
    unnamed x1, local copies, waits for them, and re-layouts  1.87 us

profile of v4, /device:TPU:5, one launch (start us, length us, event | category | flops | bytes accessed | tf_op | source)
XLA Modules:
  0.0 45.5 jit_solution(7395780681909190078)
XLA Ops:
  0.0 43.6 %shard_map.64 = bf16[1,2,256,512]{3,2,1,0:T(8,128)(2,1)} custom-call(bf16[2,256,128]{2,1,0:T(8,128)(2,1)} %features.1, bf16[128,512]{1,0:T(8,128)(2,1)} %input_weight.1, bf16[2,512,512]{2,1,0:T(8,128)(2,1)} %weights.1, bf16[2,2,4,128,128]{4,3,2,1,0:T(8,128)(2,1)} %tiles.1, s32[2,2]{1,0:T(2,128)} %pub_ids.1, s32[2,2,4]{2,1,0:T(2,128)} %tile_src.1), custom_call_target="tpu_custom_call" | custom-call | tf_op jit(solution)/shard_map/pallas_call | solution.py:404
  43.6 1.9 %copy.8 = bf16[1,2,256,512]{3,2,1,0:T(8,128)(2,1)} copy(bf16[1,2,256,512]{3,2,1,0:T(8,128)(2,1)} %shard_map.64) | data formatting | bytes 1048576

commit v5 on v4

--- a/solution.py
+++ b/solution.py
@@ -20,8 +20,8 @@
 
 
 def kernel(
-    sections, partitions, features, input_weight, weights, tiles, pub_ids, tile_src, out,
-    table, last, slab, rows_in, proj, tile_buf, near_op, ghost_op, ints, support, near_sum, ghost_sum,
+    sections, partitions, features, input_weight, weights, tiles, pub_array, src_array, out,
+    pub_ids, tile_src, table, last, slab, rows_in, proj, tile_buf, near_op, ghost_op, ints, support, near_sum, ghost_sum,
     local_sem, in_sent, feat_land, int_land, tile_land, near_sent, near_land, far_sent, far_land,
     slab_sent, slab_land, slab_pass, slab_swap, out_sent, out_land,
 ):
@@ -60,8 +60,15 @@
     tile_load = pltpu.make_async_copy(tiles.at[group], tile_buf.at[1], local_sem.at[1])
     proj_load = pltpu.make_async_copy(input_weight, proj, local_sem.at[2])
 
+    scalar_loads = (
+        pltpu.make_async_copy(pub_array, pub_ids, local_sem.at[4]),
+        pltpu.make_async_copy(src_array, tile_src, local_sem.at[5]),
+    )
+
     @pl.when(chain)
     def _():
+        for copy in scalar_loads:
+            copy.start()
         feature_load.start()
         proj_load.start()
         tile_load.start()
@@ -71,6 +78,8 @@
             pltpu.make_async_copy(src, dst, slab_land.at[layer]).start()
             src, dst = local_half(layer, 1 - core)
             pltpu.make_async_copy(src, dst, slab_swap.at[layer]).start()
+        for copy in scalar_loads:
+            copy.wait()
         row = lax.broadcasted_iota(jnp.int32, (16, 128), 0)
         packed = jnp.zeros((16, 128), jnp.int32)
         for m in range(2):
@@ -398,15 +407,20 @@
     partitions = lax.axis_size("dom")
     layers = sections * per_section
     anywhere = pl.BlockSpec(memory_space=pl.ANY)
-    scalars = pl.BlockSpec(memory_space=pltpu.SMEM)
     dma = pltpu.SemaphoreType.DMA
     bf16 = jnp.bfloat16
+    held = [
+        pltpu.with_memory_space_constraint(value, pltpu.HBM)
+        for value in (features, input_weight, layer_weights, tiles, pub_ids, tile_src)
+    ]
     return pl.pallas_call(
         functools.partial(kernel, sections, partitions),
         out_shape=jax.ShapeDtypeStruct((1, groups, rows, width), bf16),
-        in_specs=[anywhere] * 4 + [scalars] * 2,
+        in_specs=[anywhere] * 6,
         out_specs=anywhere,
         scratch_shapes=[
+            pltpu.SMEM(pub_ids.shape, jnp.int32),
+            pltpu.SMEM(tile_src.shape, jnp.int32),
             pltpu.VMEM((layers, 4 * rows, width), bf16),
             pltpu.VMEM((rows, width), bf16),
             pltpu.VMEM((layers, width, width), bf16),
@@ -419,7 +433,7 @@
             pltpu.VMEM((rows, width), bf16),
             pltpu.VMEM((rows, width), jnp.float32),
             pltpu.VMEM((rows, width), jnp.float32),
-            dma((4,)),
+            dma((6,)),
             dma((7,)),
             dma((4,)),
             dma((4,)),
@@ -435,8 +449,8 @@
             dma((sections,)),
             dma((groups,)),
         ],
-        compiler_params=pltpu.CompilerParams(collective_id=0, has_side_effects=True),
-    )(features, input_weight, layer_weights, tiles, pub_ids, tile_src)
+        compiler_params=pltpu.CompilerParams(collective_id=0, has_side_effects=True, vmem_limit_bytes=40 * 2**20),
+    )(*held)
 
 
 def solution(mesh):

time: 45.7 us -> 44.6 us (0.976)
  local copies, waits for them, and re-layouts: 1.87 us -> 0.8 us
    unnamed x1, local copies, waits for them, and re-layouts: 1.87 us -> 0.8 us
where the time goes in v5:
time: 44.6 us; the launch traced here: 44.4 us
  Pallas kernels  43.6 us (98%)
  local copies, waits for them, and re-layouts  0.8 us (2%)
    pallas_call x1, Pallas kernels, shards(): pl.pallas_call(functools.partial(kernel, sections, partitions), out_shape...  43.6 us

profile of v5, /device:TPU:5, one launch (start us, length us, event | category | flops | bytes accessed | tf_op | source)
XLA Modules:
  0.0 44.4 jit_solution(17925694131808630567)
XLA Ops:
  0.0 43.6 %shard_map.64 = bf16[1,2,256,512]{3,2,1,0:T(8,128)(2,1)S(1)} custom-call(bf16[2,256,128]{2,1,0:T(8,128)(2,1)} %features.1, bf16[128,512]{1,0:T(8,128)(2,1)} %input_weight.1, bf16[2,512,512]{2,1,0:T(8,128)(2,1)} %weights.1, bf16[2,2,4,128,128]{4,3,2,1,0:T(8,128)(2,1)} %tiles.1, s32[2,2]{1,0:T(2,128)} %pub_array.1, s32[2,2,4]{2,1,0:T(2,128)} %src_array.1), custom_call_target="tpu_custom_call" | custom-call | tf_op jit(solution)/shard_map/pallas_call | solution.py:416
  43.6 0.8 %copy.8 = bf16[1,2,256,512]{3,2,1,0:T(8,128)(2,1)} copy(bf16[1,2,256,512]{3,2,1,0:T(8,128)(2,1)S(1)} %shard_map.64) | data formatting | bytes 1048576

commit v6 on v5

--- a/solution.py
+++ b/solution.py
@@ -219,11 +219,12 @@
             op[:, rows:], table[layer, (base + 1) * rows : (base + 3) * rows, :], preferred_element_type=jnp.float32
         )
 
-    def propagate(op, layer, base, total, dst, done):
+    def propagate(op, layer, base, total, dst, done, pieces=2):
+        piece = rows // pieces
         beta = jnp.float32(0.0)
         for i in range(layers):
             beta = jnp.where(layer == i, jnp.float32(math.log(THETA / (i + 1) + 1.0)), beta)
-        for m in range(2):
+        for m in range(pieces):
             part = slice(m * piece, (m + 1) * piece)
             aggregate = total[part, :] + jnp.dot(
                 op[part, :rows], table[layer, base * rows : (base + 1) * rows, :], preferred_element_type=jnp.float32
@@ -284,26 +285,26 @@
             slab_swapped(layer)
 
             def send(m):
-                near_copy(layer + 1, m).start()
-
                 @pl.when((layer < layers - 2) & to_target)
                 def _():
                     far_copy(layer + 1, m).start()
 
+                near_copy(layer + 1, m).start()
+
+                @pl.when(lax.rem(layer + 1, per_section) == 0)
+                def _():
+                    plane = (layer + 1) // per_section - 1
+                    state = table.at[layer + 1, pl.ds(2 * rows + m * piece, piece)]
+
+                    @pl.when(plane == section)
+                    def _():
+                        out_local(state, m).start()
+
+                    @pl.when(plane != section)
+                    def _():
+                        out_copy(state, plane, m).start()
+
             propagate(near_op, layer, 1, near_sum, table.at[layer + 1, at(2)], send)
-
-            @pl.when(lax.rem(layer + 1, per_section) == 0)
-            def _():
-                plane = (layer + 1) // per_section - 1
-                state = table.at[layer + 1, at(2)]
-
-                @pl.when(plane == section)
-                def _():
-                    out_local(state).start()
-
-                @pl.when(plane != section)
-                def _():
-                    out_copy(state, plane).start()
 
             slab_ready(layer + 1)
 
@@ -327,7 +328,7 @@
 
             @pl.when(inner)
             def _():
-                propagate(ghost_op, layer, 0, ghost_sum, table.at[layer + 1, at(1)], lambda m: None)
+                propagate(ghost_op, layer, 0, ghost_sum, table.at[layer + 1, at(1)], lambda m: None, 1)
 
             return carry
 

time: 44.6 us -> 44 us (0.987)
  Pallas kernels: 43.6 us -> 43 us
    pallas_call x1, Pallas kernels: 43.6 us -> 43 us  [shards(): pl.pallas_call(functools.partial(kernel, sections, partitions), out_shape...]
where the time goes in v6:
time: 44 us; the launch traced here: 43.8 us
  Pallas kernels  43 us (98%)
  local copies, waits for them, and re-layouts  0.8 us (2%)
    pallas_call x1, Pallas kernels, shards(): pl.pallas_call(functools.partial(kernel, sections, partitions), out_shape...  43 us

profile of v6, /device:TPU:5, one launch (start us, length us, event | category | flops | bytes accessed | tf_op | source)
XLA Modules:
  0.0 43.8 jit_solution(17749841950261194318)
XLA Ops:
  0.0 43.0 %shard_map.64 = bf16[1,2,256,512]{3,2,1,0:T(8,128)(2,1)S(1)} custom-call(bf16[2,256,128]{2,1,0:T(8,128)(2,1)} %features.1, bf16[128,512]{1,0:T(8,128)(2,1)} %input_weight.1, bf16[2,512,512]{2,1,0:T(8,128)(2,1)} %weights.1, bf16[2,2,4,128,128]{4,3,2,1,0:T(8,128)(2,1)} %tiles.1, s32[2,2]{1,0:T(2,128)} %pub_array.1, s32[2,2,4]{2,1,0:T(2,128)} %src_array.1), custom_call_target="tpu_custom_call" | custom-call | tf_op jit(solution)/shard_map/pallas_call | solution.py:417
  43.0 0.8 %copy.8 = bf16[1,2,256,512]{3,2,1,0:T(8,128)(2,1)} copy(bf16[1,2,256,512]{3,2,1,0:T(8,128)(2,1)S(1)} %shard_map.64) | data formatting | bytes 1048576
